TPU v7x, 512 devices: a whole 4x8x8 slice. The times are simulated.
512 devices in a mesh: dp: 128 (over y, z, core), grp: 4 (over x).
Axes of the slice: x: 4, y: 8, z: 8, core: 2. Of those that a mesh axis runs over, the one named last changes fastest.
Arguments:
- states: bfloat16 [65536, 2048], P(('dp', 'grp')), may hold values from -60 to 60
- projection: bfloat16 [2048, 768], replicated, may hold values from -0.125 to 0.125
- owner_group: int32 [65536, 1], P(('dp', 'grp')), may hold values from 0 to 127; in each aligned block of 128 rows (0 to 127, 128 to 255, ...) at most 2 rows name the same one
- cluster_sub: int32 [65536], P(('dp', 'grp')), may hold values from 0 to 3
- priority: int32 [65536], P(('dp', 'grp')), may hold values from 0 to 65535, each once
Outputs:
- dup_score: float32 [65536], P(('dp', 'grp'))
Inputs may be any that keep to these rules, and one draw needn't show every extreme that they name: `owner_group`: in each aligned block of 128 rows (the rows of one device) no owner is named by more than 2 rows; in some block some owner is named by exactly 2 rows.
All inputs are finite; a program needn't handle non-finite values.
Results may differ from a plain program's by a relative error of at most 0.0012.
Values may be sent and summed in bfloat16 or wider, within the bound.
A program may use at most 64 MiB of HBM per device.

v0:
```python
import jax
import jax.numpy as jnp
from jax import lax
from jax.sharding import PartitionSpec as P


def pair_tile(query_emb, key_emb):
    return lax.dot_general(
        query_emb, key_emb, (((1,), (1,)), ((), ())), preferred_element_type=jnp.float32
    )


def on_device(states, projection, owner_group, cluster_sub, priority):
    num_dp = lax.axis_size("dp")
    doc_rows = states.shape[0]
    emb_width = projection.shape[1]
    slot_count = max(2, (2 * doc_rows + num_dp - 1) // num_dp)
    recv_rows = num_dp * slot_count
    projected = jnp.dot(states, projection, preferred_element_type=jnp.float32)
    square_sum = jnp.sum(projected * projected, axis=1, keepdims=True)
    inverse_norm = lax.rsqrt(square_sum + 1e-06)
    embedding = (projected * inverse_norm).astype(jnp.bfloat16)
    owner_row = owner_group[:, 0]
    onehot = (owner_row[:, None] == jnp.arange(num_dp, dtype=jnp.int32)[None, :]).astype(jnp.int32)
    slot_place = jnp.sum(onehot * (jnp.cumsum(onehot, axis=0) - 1), axis=1)
    target = owner_row * slot_count + slot_place
    send_emb = jnp.zeros((recv_rows, emb_width), jnp.bfloat16).at[target].set(embedding)
    send_sub = jnp.full((recv_rows,), -1, jnp.int32).at[target].set(cluster_sub)
    send_prio = jnp.zeros((recv_rows,), jnp.int32).at[target].set(priority)
    got_emb, got_sub, got_prio = (
        lax.all_to_all(
            send_emb.reshape(num_dp, slot_count, emb_width),
            "dp",
            split_axis=0,
            concat_axis=0,
            tiled=True,
        ),
        lax.all_to_all(
            send_sub.reshape(num_dp, slot_count), "dp", split_axis=0, concat_axis=0, tiled=True
        ),
        lax.all_to_all(
            send_prio.reshape(num_dp, slot_count), "dp", split_axis=0, concat_axis=0, tiled=True
        ),
    )
    member_emb = got_emb.reshape(recv_rows, emb_width)
    member_sub = got_sub.reshape(recv_rows)
    member_prio = got_prio.reshape(recv_rows)
    lowest = jnp.full((recv_rows,), -1.0, jnp.float32)
    cosine = pair_tile(member_emb, lax.all_gather(member_emb, "grp", axis=0, tiled=True))
    earlier = (
        member_sub[:, None] == lax.all_gather(member_sub, "grp", axis=0, tiled=True)[None, :]
    ) & (lax.all_gather(member_prio, "grp", axis=0, tiled=True)[None, :] < member_prio[:, None])
    running = jnp.maximum(lowest, jnp.max(jnp.where(earlier, cosine, -1.0), axis=1))
    result_back = lax.all_to_all(
        running.reshape(num_dp, slot_count), "dp", split_axis=0, concat_axis=0, tiled=True
    )
    return result_back.reshape(recv_rows)[target]


def solution(mesh):
    in_specs = (
        P(("dp", "grp"), None),
        P(),
        P(("dp", "grp"), None),
        P(("dp", "grp")),
        P(("dp", "grp")),
    )
    out_specs = P(("dp", "grp"))
    return jax.shard_map(
        on_device, mesh=mesh, in_specs=in_specs, out_specs=out_specs, check_vma=False
    )
```

profile of v0, /device:TPU:1, one launch (start us, length us, event | category | flops | bytes accessed | tf_op | source)
XLA Modules:
  0.0 138.6 jit_solution(18221700818211266229)
XLA Ops:
  6.5 0.9 fusion.4
  7.4 0.2 reduce_window_sum.11
  7.6 0.8 select_reduce_fusion
  8.4 0.7 fusion.5
  9.1 1.7 %multiply_reduce_fusion = (f32[128]{0:T(128)S(1)}, f32[128,768]{1,0:T(8,128)S(1)}) fusion(bf16[128,2048]{1,0:T(8,128)(2,1)} %param.5, bf16[2048,768]{1,0:T(8,128)(2,1)S(1)} %copy-done), kind=kOutput, calls=%fused_computation.7 | convolution fusion | flops 402849664 | bytes 4063744 | tf_op jit(solution)/shard_map/dot_general | solution.py:19
  10.8 1.9 %scatter_custom_fusion.2 = bf16[256,768]{1,0:T(8,128)(2,1)} fusion(s32[128]{0:T(128)S(1)} %fusion.5, f32[128,768]{1,0:T(8,128)S(1)} %get-tuple-element.6, f32[128]{0:T(128)S(1)} %add_rsqrt_fusion, bf16[]{:T(256)} %constant.13.clone.1), kind=kCustom, calls=%fused_computation.8 | custom fusion | flops 196608 | bytes 786946 | tf_op jit(solution)/shard_map/scatter | solution.py:27
  12.7 1.1 reshape.54
  13.9 35.1 %all_to_all.29 = bf16[128,2,768]{2,1,0:T(2,128)(2,1)} all-to-all(bf16[128,2,768]{2,1,0:T(2,128)(2,1)S(1)} %reshape.54), channel_id=1, replica_groups=mesh['dp'=128,'grp'=4] {'dp'}, dimensions={0} | all-to-all | bytes 786432 | tf_op jit(solution)/shard_map/all_to_all | solution.py:31
  49.0 1.9 %reshape.55 = bf16[256,768]{1,0:T(8,128)(2,1)} reshape(bf16[128,2,768]{2,1,0:T(2,128)(2,1)} %all_to_all.29) | data formatting | bytes 786432 | tf_op jit(solution)/shard_map/reshape | solution.py:45
  50.9 1.1 scatter_custom_fusion
  52.0 0.8 all_to_all.19
  52.8 7.1 %all-to-all-start = ((s32[128,1,2]{2,1,0:T(1,128)}), s32[128,1,2]{2,1,0:T(1,128)S(1)}, u32[]{:S(2)}, u32[]{:S(2)}) async-start(s32[128,1,2]{2,1,0:T(1,128)} %bitcast.3), calls=%async_computation | async-start | bytes 131072 | tf_op jit(solution)/shard_map/all_to_all | solution.py:38
  59.9 1.1 scatter_custom_fusion.1
  61.0 0.8 all_to_all.21
  61.8 9.8 %all-to-all-done = s32[128,1,2]{2,1,0:T(1,128)S(1)} async-done(((s32[128,1,2]{2,1,0:T(1,128)}), s32[128,1,2]{2,1,0:T(1,128)S(1)}, u32[]{:S(2)}, u32[]{:S(2)}) %all-to-all-start) | async-done | bytes 1056 | tf_op jit(solution)/shard_map/all_to_all | solution.py:38
  71.6 5.7 %all-to-all-start.1 = ((s32[128,1,2]{2,1,0:T(1,128)}), s32[128,1,2]{2,1,0:T(1,128)S(1)}, u32[]{:S(2)}, u32[]{:S(2)}) async-start(s32[128,1,2]{2,1,0:T(1,128)} %bitcast.5), calls=%async_computation.1 | async-start | bytes 131072 | tf_op jit(solution)/shard_map/all_to_all | solution.py:41
  77.2 0.1 reshape.89
  77.4 11.5 %all-to-all-done.1 = s32[128,1,2]{2,1,0:T(1,128)S(1)} async-done(((s32[128,1,2]{2,1,0:T(1,128)}), s32[128,1,2]{2,1,0:T(1,128)S(1)}, u32[]{:S(2)}, u32[]{:S(2)}) %all-to-all-start.1) | async-done | bytes 1056 | tf_op jit(solution)/shard_map/all_to_all | solution.py:41
  89.0 0.5 broadcast.57
  89.5 0.8 reduce.13
  90.3 0.1 reshape.91
  90.5 0.8 reduce.14
  91.3 0.1 eq.34
  91.4 7.7 %all-gather = s32[4,1,256]{2,1,0:T(1,128)S(1)} all-gather(s32[1,1,256]{2,1,0:T(1,128)S(1)} %reshape.89), channel_id=1, replica_groups=mesh['dp'=128,'grp'=4] {'grp'}, dimensions={0}, use_global_device_ids=true | all-gather | bytes 5120 | tf_op jit(solution)/shard_map/all_gather | solution.py:51
  99.1 5.2 %all-gather.1 = s32[4,1,256]{2,1,0:T(1,128)S(1)} all-gather(s32[1,1,256]{2,1,0:T(1,128)S(1)} %reshape.91), channel_id=1, replica_groups=mesh['dp'=128,'grp'=4] {'grp'}, dimensions={0}, use_global_device_ids=true | all-gather | bytes 5120 | tf_op jit(solution)/shard_map/all_gather | solution.py:52
  104.3 2.3 %fusion = f32[256]{0:T(256)S(1)} fusion(bf16[256,768]{1,0:T(8,128)(2,1)} %reshape.55, bf16[1024,768]{1,0:T(8,128)(2,1)} %all-gather.4.cloned.1.call-done, s32[1024]{0:T(1024)S(1)} %bitcast.24, s32[1024]{0:T(1024)S(1)} %bitcast.23, s32[256]{0:T(256)S(1)} %reshape.53, s32[256]{0:T(256)S(1)} %eq.34), kind=kOutput, calls=%fused_computation.5 | convolution fusion | flops 403963648 | bytes 1977344 | tf_op jit(solution)/shard_map/dot_general | solution.py:8
  106.6 0.8 max_broadcast_in_dim.15
  107.4 9.5 %all-to-all-start.3 = ((f32[128,1,2]{2,1,0:T(1,128)}), f32[128,1,2]{2,1,0:T(1,128)S(1)}, u32[]{:S(2)}, u32[]{:S(2)}) async-start(f32[128,1,2]{2,1,0:T(1,128)} %bitcast.7), calls=%async_computation.3 | async-start | bytes 131072 | tf_op jit(solution)/shard_map/all_to_all | solution.py:54
  116.9 11.6 %all-to-all-done.3 = f32[128,1,2]{2,1,0:T(1,128)S(1)} async-done(((f32[128,1,2]{2,1,0:T(1,128)}), f32[128,1,2]{2,1,0:T(1,128)S(1)}, u32[]{:S(2)}, u32[]{:S(2)}) %all-to-all-start.3) | async-done | bytes 1056 | tf_op jit(solution)/shard_map/all_to_all | solution.py:54
  128.5 0.5 broadcast.59
  129.0 0.8 reduce.15
  130.0 1.8 %gather_fusion = f32[128]{0:T(128)} fusion(f32[256]{0:T(256)S(1)} %reshape.56, s32[1024]{0:T(1024)S(1)} %pad_clamp_fusion), kind=kCustom, calls=%fused_computation | custom fusion | bytes 1536 | tf_op jit(solution)/shard_map/gather | solution.py:57
  (10 shorter events, 0.3 us)
Async XLA Ops:
  6.5 2.6 %copy-start = (bf16[2048,768]{1,0:T(8,128)(2,1)S(1)}, bf16[2048,768]{1,0:T(8,128)(2,1)}, u32[]{:S(2)}) copy-start(bf16[2048,768]{1,0:T(8,128)(2,1)} %param.6) | copy-start | bytes 9437188
  6.5 97.8 %all-gather.4.cloned.1.call-start = ((), (), s32[]{:S(2)}) async-start(), calls=%async_computation.4 | async-start | bytes 1966080 | tf_op jit(solution)/shard_map/all_gather | solution.py:49
  52.8 18.8 %all-to-all-start = ((s32[128,1,2]{2,1,0:T(1,128)}), s32[128,1,2]{2,1,0:T(1,128)S(1)}, u32[]{:S(2)}, u32[]{:S(2)}) async-start(s32[128,1,2]{2,1,0:T(1,128)} %bitcast.3), calls=%async_computation | async-start | bytes 131072 | tf_op jit(solution)/shard_map/all_to_all | solution.py:38
  71.6 17.3 %all-to-all-start.1 = ((s32[128,1,2]{2,1,0:T(1,128)}), s32[128,1,2]{2,1,0:T(1,128)S(1)}, u32[]{:S(2)}, u32[]{:S(2)}) async-start(s32[128,1,2]{2,1,0:T(1,128)} %bitcast.5), calls=%async_computation.1 | async-start | bytes 131072 | tf_op jit(solution)/shard_map/all_to_all | solution.py:41
  107.4 21.1 %all-to-all-start.3 = ((f32[128,1,2]{2,1,0:T(1,128)}), f32[128,1,2]{2,1,0:T(1,128)S(1)}, u32[]{:S(2)}, u32[]{:S(2)}) async-start(f32[128,1,2]{2,1,0:T(1,128)} %bitcast.7), calls=%async_computation.3 | async-start | bytes 131072 | tf_op jit(solution)/shard_map/all_to_all | solution.py:54
Sparse Core Ops, SparseCore 0:
  51.0 25.2 all-gather.3
where the time goes:
time: 139 us
  blocking collectives  48.1 us (35%)
  waiting for transfers between devices  32.9 us (24%)
  starting transfers between devices  22.3 us (16%)
  between operations  13.5 us (10%)
  local copies, waits for them, and re-layouts  11 us (8%)
  other arithmetic  6.92 us (5%)
  matrix products  3.96 us (3%)
    all_to_all x1, blocking collectives, on_device(): lax.all_to_all(send_emb.reshape(num_dp, slot_count, emb_width), 'dp', spl...  35.1 us
    all_to_all x1, waiting for transfers between devices, on_device(): lax.all_to_all(running.reshape(num_dp, slot_count), 'dp', split_axis=0, c...  11.6 us
    all_to_all x1, waiting for transfers between devices, on_device(): lax.all_to_all(send_prio.reshape(num_dp, slot_count), 'dp', split_axis=0,...  11.5 us
    all_to_all x1, waiting for transfers between devices, on_device(): lax.all_to_all(send_sub.reshape(num_dp, slot_count), 'dp', split_axis=0,...  9.76 us
    all_to_all x1, starting transfers between devices, on_device(): lax.all_to_all(running.reshape(num_dp, slot_count), 'dp', split_axis=0, c...  9.48 us
    all_gather x1, blocking collectives, on_device(): lax.all_gather(member_sub, 'grp', axis=0, tiled=True)[None, :]  7.71 us
    all_to_all x1, starting transfers between devices, on_device(): lax.all_to_all(send_sub.reshape(num_dp, slot_count), 'dp', split_axis=0,...  7.12 us
    all_to_all x1, starting transfers between devices, on_device(): lax.all_to_all(send_prio.reshape(num_dp, slot_count), 'dp', split_axis=0,...  5.65 us
  transfers between devices with their start and end apart: 4, of which 3 were waited for; matrix products, arithmetic and copies ran while one was open for 4% of the time, Pallas kernels for 0%

commit v1 on v0

--- a/solution.py
+++ b/solution.py
@@ -2,6 +2,11 @@
 import jax.numpy as jnp
 from jax import lax
 from jax.sharding import PartitionSpec as P
+
+
+def gather_from_all(x, axis, dim):
+    copies = jnp.concatenate([x] * lax.axis_size(axis), axis=dim)
+    return lax.all_to_all(copies, axis, dim, dim, tiled=True)
 
 
 def pair_tile(query_emb, key_emb):
@@ -47,9 +52,9 @@
     member_prio = got_prio.reshape(recv_rows)
     lowest = jnp.full((recv_rows,), -1.0, jnp.float32)
     cosine = pair_tile(member_emb, lax.all_gather(member_emb, "grp", axis=0, tiled=True))
-    earlier = (
-        member_sub[:, None] == lax.all_gather(member_sub, "grp", axis=0, tiled=True)[None, :]
-    ) & (lax.all_gather(member_prio, "grp", axis=0, tiled=True)[None, :] < member_prio[:, None])
+    earlier = (member_sub[:, None] == gather_from_all(member_sub, "grp", 0)[None, :]) & (
+        lax.all_gather(member_prio, "grp", axis=0, tiled=True)[None, :] < member_prio[:, None]
+    )
     running = jnp.maximum(lowest, jnp.max(jnp.where(earlier, cosine, -1.0), axis=1))
     result_back = lax.all_to_all(
         running.reshape(num_dp, slot_count), "dp", split_axis=0, concat_axis=0, tiled=True

time: 139 us -> 136 us (0.978)
  blocking collectives: 48.1 us -> 43 us
  starting transfers between devices: 22.3 us -> 25.1 us
    all_gather x1 -> x0, blocking collectives: 7.71 us -> none  [on_device(): lax.all_gather(member_sub, 'grp', axis=0, tiled=True)[None, :]]
    all_to_all x0 -> x1, starting transfers between devices: none -> 4.02 us  [gather_from_all(): return lax.all_to_all(copies, axis, dim, dim, tiled=True)]
    all_gather x1, blocking collectives: 5.23 us -> 7.9 us  [on_device(): lax.all_gather(member_prio, 'grp', axis=0, tiled=True)[None, :]]
  transfers between devices with their start and end apart: 4 -> 5, of which waited for: 3 -> 3; matrix products, arithmetic and copies ran while one was open for 4% -> 4% of each run, Pallas kernels for 0% -> 0%
where the time goes in v1:
time: 136 us
  blocking collectives  43 us (32%)
  waiting for transfers between devices  31.6 us (23%)
  starting transfers between devices  25.1 us (18%)
  between operations  13.5 us (10%)
  local copies, waits for them, and re-layouts  11.5 us (8%)
  other arithmetic  6.92 us (5%)
  matrix products  3.96 us (3%)
    all_to_all x1, blocking collectives, on_device(): lax.all_to_all(send_emb.reshape(num_dp, slot_count, emb_width), 'dp', spl...  35.1 us
    all_to_all x1, waiting for transfers between devices, on_device(): lax.all_to_all(running.reshape(num_dp, slot_count), 'dp', split_axis=0, c...  11.6 us
    all_to_all x1, waiting for transfers between devices, on_device(): lax.all_to_all(send_prio.reshape(num_dp, slot_count), 'dp', split_axis=0,...  10.2 us
    all_to_all x1, waiting for transfers between devices, on_device(): lax.all_to_all(send_sub.reshape(num_dp, slot_count), 'dp', split_axis=0,...  9.76 us
    all_to_all x1, starting transfers between devices, on_device(): lax.all_to_all(running.reshape(num_dp, slot_count), 'dp', split_axis=0, c...  8.31 us
    all_gather x1, blocking collectives, on_device(): lax.all_gather(member_prio, 'grp', axis=0, tiled=True)[None, :]  7.9 us
    all_to_all x1, starting transfers between devices, on_device(): lax.all_to_all(send_sub.reshape(num_dp, slot_count), 'dp', split_axis=0,...  7.12 us
    all_to_all x1, starting transfers between devices, on_device(): lax.all_to_all(send_prio.reshape(num_dp, slot_count), 'dp', split_axis=0,...  5.65 us
  transfers between devices with their start and end apart: 5, of which 3 were waited for; matrix products, arithmetic and copies ran while one was open for 4% of the time, Pallas kernels for 0%

profile of v1, /device:TPU:1, one launch (start us, length us, event | category | flops | bytes accessed | tf_op | source)
XLA Modules:
  0.0 135.5 jit_solution(10363941797466229855)
XLA Ops:
  6.5 0.9 fusion.4
  7.4 0.2 reduce_window_sum.11
  7.6 0.8 select_reduce_fusion
  8.4 0.7 fusion.5
  9.1 1.7 %multiply_reduce_fusion = (f32[128]{0:T(128)S(1)}, f32[128,768]{1,0:T(8,128)S(1)}) fusion(bf16[128,2048]{1,0:T(8,128)(2,1)} %param.5, bf16[2048,768]{1,0:T(8,128)(2,1)S(1)} %copy-done), kind=kOutput, calls=%fused_computation.7 | convolution fusion | flops 402849664 | bytes 4063744 | tf_op jit(solution)/shard_map/dot_general | solution.py:24
  10.8 1.9 %scatter_custom_fusion.2 = bf16[256,768]{1,0:T(8,128)(2,1)} fusion(s32[128]{0:T(128)S(1)} %fusion.5, f32[128,768]{1,0:T(8,128)S(1)} %get-tuple-element.6, f32[128]{0:T(128)S(1)} %add_rsqrt_fusion, bf16[]{:T(256)} %constant.13.clone.1), kind=kCustom, calls=%fused_computation.8 | custom fusion | flops 196608 | bytes 786946 | tf_op jit(solution)/shard_map/scatter | solution.py:32
  12.7 1.1 reshape.69
  13.9 35.1 %all_to_all.35 = bf16[128,2,768]{2,1,0:T(2,128)(2,1)} all-to-all(bf16[128,2,768]{2,1,0:T(2,128)(2,1)S(1)} %reshape.69), channel_id=1, replica_groups=mesh['dp'=128,'grp'=4] {'dp'}, dimensions={0} | all-to-all | bytes 786432 | tf_op jit(solution)/shard_map/all_to_all | solution.py:36
  49.0 1.9 %reshape.70 = bf16[256,768]{1,0:T(8,128)(2,1)} reshape(bf16[128,2,768]{2,1,0:T(2,128)(2,1)} %all_to_all.35) | data formatting | bytes 786432 | tf_op jit(solution)/shard_map/reshape | solution.py:50
  50.9 1.1 scatter_custom_fusion
  52.0 0.8 all_to_all.23
  52.8 7.1 %all-to-all-start = ((s32[128,1,2]{2,1,0:T(1,128)}), s32[128,1,2]{2,1,0:T(1,128)S(1)}, u32[]{:S(2)}, u32[]{:S(2)}) async-start(s32[128,1,2]{2,1,0:T(1,128)} %bitcast.3), calls=%async_computation | async-start | bytes 131072 | tf_op jit(solution)/shard_map/all_to_all | solution.py:43
  59.9 1.1 scatter_custom_fusion.1
  61.0 0.8 all_to_all.26
  61.8 9.8 %all-to-all-done = s32[128,1,2]{2,1,0:T(1,128)S(1)} async-done(((s32[128,1,2]{2,1,0:T(1,128)}), s32[128,1,2]{2,1,0:T(1,128)S(1)}, u32[]{:S(2)}, u32[]{:S(2)}) %all-to-all-start) | async-done | bytes 1056 | tf_op jit(solution)/shard_map/all_to_all | solution.py:43
  71.6 5.7 %all-to-all-start.2 = ((s32[128,1,2]{2,1,0:T(1,128)}), s32[128,1,2]{2,1,0:T(1,128)S(1)}, u32[]{:S(2)}, u32[]{:S(2)}) async-start(s32[128,1,2]{2,1,0:T(1,128)} %bitcast.5), calls=%async_computation.2 | async-start | bytes 131072 | tf_op jit(solution)/shard_map/all_to_all | solution.py:46
  77.2 0.5 broadcast.56
  77.7 0.8 reduce.12
  78.6 0.1 eq.36
  78.7 10.2 %all-to-all-done.2 = s32[128,1,2]{2,1,0:T(1,128)S(1)} async-done(((s32[128,1,2]{2,1,0:T(1,128)}), s32[128,1,2]{2,1,0:T(1,128)S(1)}, u32[]{:S(2)}, u32[]{:S(2)}) %all-to-all-start.2) | async-done | bytes 1056 | tf_op jit(solution)/shard_map/all_to_all | solution.py:46
  88.8 0.6 concatenate.4
  89.4 4.0 %all-to-all-start.1 = ((s32[4,256,1]{1,2,0:T(1,128)}), s32[4,256,1]{1,2,0:T(1,128)S(1)}, u32[]{:S(2)}, u32[]{:S(2)}) async-start(s32[4,256,1]{1,2,0:T(1,128)} %concatenate.4), calls=%async_computation.1 | async-start | bytes 8192 | tf_op jit(solution)/shard_map/all_to_all | solution.py:9
  93.6 0.8 reduce.11
  94.4 0.1 reshape.104
  94.6 7.9 %all-gather = s32[4,1,256]{2,1,0:T(1,128)S(1)} all-gather(s32[1,1,256]{2,1,0:T(1,128)S(1)} %reshape.104), channel_id=1, replica_groups=mesh['dp'=128,'grp'=4] {'grp'}, dimensions={0}, use_global_device_ids=true | all-gather | bytes 5120 | tf_op jit(solution)/shard_map/all_gather | solution.py:56
  102.5 2.3 %fusion = f32[256]{0:T(256)S(1)} fusion(bf16[256,768]{1,0:T(8,128)(2,1)} %reshape.70, bf16[1024,768]{1,0:T(8,128)(2,1)} %all-gather.3.cloned.1.call-done, s32[1024]{0:T(1024)S(1)} %bitcast.21, s32[1024]{0:T(1024)S(1)} %bitcast.22, s32[256]{0:T(256)S(1)} %reshape.68, s32[256]{0:T(256)S(1)} %eq.36), kind=kOutput, calls=%fused_computation.5 | convolution fusion | flops 403963648 | bytes 1977344 | tf_op jit(solution)/shard_map/dot_general | solution.py:13
  104.7 0.8 max_broadcast_in_dim.15
  105.5 8.3 %all-to-all-start.4 = ((f32[128,1,2]{2,1,0:T(1,128)}), f32[128,1,2]{2,1,0:T(1,128)S(1)}, u32[]{:S(2)}, u32[]{:S(2)}) async-start(f32[128,1,2]{2,1,0:T(1,128)} %bitcast.7), calls=%async_computation.4 | async-start | bytes 131072 | tf_op jit(solution)/shard_map/all_to_all | solution.py:59
  113.8 11.6 %all-to-all-done.4 = f32[128,1,2]{2,1,0:T(1,128)S(1)} async-done(((f32[128,1,2]{2,1,0:T(1,128)}), f32[128,1,2]{2,1,0:T(1,128)S(1)}, u32[]{:S(2)}, u32[]{:S(2)}) %all-to-all-start.4) | async-done | bytes 1056 | tf_op jit(solution)/shard_map/all_to_all | solution.py:59
  125.5 0.5 broadcast.58
  126.0 0.8 reduce.13
  126.9 1.8 %gather_fusion = f32[128]{0:T(128)} fusion(f32[256]{0:T(256)S(1)} %reshape.71, s32[1024]{0:T(1024)S(1)} %pad_clamp_fusion), kind=kCustom, calls=%fused_computation | custom fusion | bytes 1536 | tf_op jit(solution)/shard_map/gather | solution.py:62
  (11 shorter events, 0.3 us)
Async XLA Ops:
  6.5 2.6 %copy-start = (bf16[2048,768]{1,0:T(8,128)(2,1)S(1)}, bf16[2048,768]{1,0:T(8,128)(2,1)}, u32[]{:S(2)}) copy-start(bf16[2048,768]{1,0:T(8,128)(2,1)} %param.6) | copy-start | bytes 9437188
  6.5 95.9 %all-gather.3.cloned.1.call-start = ((), (), s32[]{:S(2)}) async-start(), calls=%async_computation.5 | async-start | bytes 1966080 | tf_op jit(solution)/shard_map/all_gather | solution.py:54
  52.8 18.8 %all-to-all-start = ((s32[128,1,2]{2,1,0:T(1,128)}), s32[128,1,2]{2,1,0:T(1,128)S(1)}, u32[]{:S(2)}, u32[]{:S(2)}) async-start(s32[128,1,2]{2,1,0:T(1,128)} %bitcast.3), calls=%async_computation | async-start | bytes 131072 | tf_op jit(solution)/shard_map/all_to_all | solution.py:43
  71.6 17.3 %all-to-all-start.2 = ((s32[128,1,2]{2,1,0:T(1,128)}), s32[128,1,2]{2,1,0:T(1,128)S(1)}, u32[]{:S(2)}, u32[]{:S(2)}) async-start(s32[128,1,2]{2,1,0:T(1,128)} %bitcast.5), calls=%async_computation.2 | async-start | bytes 131072 | tf_op jit(solution)/shard_map/all_to_all | solution.py:46
  89.4 13.0 %all-to-all-start.1 = ((s32[4,256,1]{1,2,0:T(1,128)}), s32[4,256,1]{1,2,0:T(1,128)S(1)}, u32[]{:S(2)}, u32[]{:S(2)}) async-start(s32[4,256,1]{1,2,0:T(1,128)} %concatenate.4), calls=%async_computation.1 | async-start | bytes 8192 | tf_op jit(solution)/shard_map/all_to_all | solution.py:9
  105.5 20.0 %all-to-all-start.4 = ((f32[128,1,2]{2,1,0:T(1,128)}), f32[128,1,2]{2,1,0:T(1,128)S(1)}, u32[]{:S(2)}, u32[]{:S(2)}) async-start(f32[128,1,2]{2,1,0:T(1,128)} %bitcast.7), calls=%async_computation.4 | async-start | bytes 131072 | tf_op jit(solution)/shard_map/all_to_all | solution.py:59
Sparse Core Ops, SparseCore 0:
  51.0 25.2 all-gather.2
